TPU v7x, 32 devices: a whole 2x2x4 slice. The times are simulated.
32 devices in a mesh: ctx: 16 (over z, y, core), tp: 2 (over x).
Axes of the slice: x: 2, y: 2, z: 4, core: 2. Of those that a mesh axis runs over, the one named last changes fastest.
Arguments:
- activations: bfloat16 [2048, 4096], P(('ctx', 'tp')), may hold values from -24 to 24
- query_weight: bfloat16 [4096, 4096], P(None, 'tp'), may hold values from -0.09375 to 0.09375
- key_weight: bfloat16 [4096, 1024], P(None, 'tp'), may hold values from -0.09375 to 0.09375
- value_weight: bfloat16 [4096, 1024], P(None, 'tp'), may hold values from -0.09375 to 0.09375
Outputs:
- attended: bfloat16 [2048, 4096], P('ctx', 'tp')
All inputs are finite; a program needn't handle non-finite values.
Results may differ from a plain program's by a relative error of at most 0.012.
The roundings to bfloat16 on the way count: a program that leaves them out, or rounds other values in their place, can miss the bound.
Values may be sent and summed in bfloat16 or wider, within the bound.
No kernel may reach another device: no remote copies, remote signals or barrier semaphores. Data moves between devices by JAX's collectives and lax.ppermute only.
A program may use at most 128 MiB of HBM per device.

v0:
```python
import math
import jax
import jax.numpy as jnp
from jax import lax
from jax.sharding import PartitionSpec as P

HD = 128
THETA = 500000.0
NEGATIVE = -1e30


def rotate(heads_in, positions):
    width = heads_in.shape[-1]
    half_width = width // 2
    frequency = THETA ** (-(jnp.arange(half_width).astype(jnp.float32) * 2.0 / width))
    angles = positions[:, None] * frequency[None, :]
    cosine = jnp.cos(angles)[:, None, :]
    sine_table = jnp.sin(angles)[:, None, :]
    front_half = heads_in[..., :half_width]
    back_half = heads_in[..., half_width:]
    return jnp.concatenate(
        [
            front_half * cosine - back_half * sine_table,
            back_half * cosine + front_half * sine_table,
        ],
        axis=-1,
    )


def block_update(state, query_block, query_pos, key_block, value_block, key_pos):
    row_top, totals, accum = state
    scale = 1.0 / math.sqrt(query_block.shape[-1])
    scores = (
        lax.dot_general(
            query_block, key_block, (((1,), (1,)), ((), ())), preferred_element_type=jnp.float32
        )
        * scale
    )
    allowed = key_pos[None, :] <= query_pos[:, None]
    block_top = jnp.max(jnp.where(allowed, scores, NEGATIVE), axis=1)
    new_top = jnp.maximum(row_top, block_top)
    correction = jnp.exp(row_top - new_top)
    weights = jnp.where(allowed, jnp.exp(scores - new_top[:, None]), 0.0)
    totals = totals * correction + jnp.sum(weights, axis=1)
    accum = accum * correction[:, None] + jnp.dot(
        weights.astype(jnp.bfloat16), value_block, preferred_element_type=jnp.float32
    )
    return (new_top, totals, accum)


def attend(groups, keys, values):
    carry_start = []
    for query_rows, query_pos, kv_slot, query_step in groups:
        row_count = query_rows.shape[0]
        blocks_count = row_count // query_step
        carry_start.append(
            (
                jnp.full((blocks_count, query_step), NEGATIVE, jnp.float32),
                jnp.zeros((blocks_count, query_step), jnp.float32),
                jnp.zeros((blocks_count, query_step, HD), jnp.float32),
            )
        )
    carry = tuple(carry_start)
    key_piece = lax.all_gather(keys, "ctx", axis=0, tiled=True)
    value_piece = lax.all_gather(values, "ctx", axis=0, tiled=True)
    piece_rows = key_piece.shape[0]
    key_step = math.gcd(piece_rows, 512)
    updated = []
    for (query_rows, query_pos, kv_slot, query_step), fold_state in zip(groups, carry):
        key_chosen = lax.dynamic_index_in_dim(
            key_piece.reshape(piece_rows, -1, HD), kv_slot, 1, keepdims=False
        )
        value_chosen = lax.dynamic_index_in_dim(
            value_piece.reshape(piece_rows, -1, HD), kv_slot, 1, keepdims=False
        )
        key_blocks = key_chosen.reshape(piece_rows // key_step, key_step, HD)
        value_blocks = value_chosen.reshape(piece_rows // key_step, key_step, HD)
        block_starts = jnp.arange(piece_rows // key_step, dtype=jnp.int32) * key_step
        blocks_count = fold_state[0].shape[0]
        query_blocks = query_rows.reshape(blocks_count, query_step, HD)
        pos_blocks = query_pos.reshape(blocks_count, query_step)

        def per_query(items):
            query_block, pos_block, row_top, totals, accum = items
            last_pos = jnp.max(pos_block)

            def per_key(inner, key_items):
                key_block, value_block, key_start = key_items
                key_pos = key_start + jnp.arange(key_step, dtype=jnp.int32)
                result = lax.cond(
                    key_start <= last_pos,
                    lambda current: block_update(
                        current, query_block, pos_block, key_block, value_block, key_pos
                    ),
                    lambda current: current,
                    inner,
                )
                return (result, None)

            final, unused = lax.scan(
                per_key, (row_top, totals, accum), (key_blocks, value_blocks, block_starts)
            )
            return final

        updated.append(
            lax.map(
                per_query, (query_blocks, pos_blocks, fold_state[0], fold_state[1], fold_state[2])
            )
        )
    final_state = tuple(updated)
    results = []
    for state in final_state:
        outcome = state[2] / state[1][..., None]
        results.append(outcome.reshape(-1, HD))
    return results


def local(activations, query_weight, key_weight, value_weight):
    tensor_count = lax.axis_size("tp")
    context_index = lax.axis_index("ctx")
    local_rows = activations.shape[0] * tensor_count
    heads_here = query_weight.shape[1] // HD
    kv_here = key_weight.shape[1] // HD
    group = heads_here // kv_here
    query_width = heads_here * HD
    key_width = kv_here * HD
    gathered = lax.all_gather(activations, "tp", axis=0, tiled=True)
    projected = jnp.concatenate(
        [
            jnp.dot(gathered, query_weight, preferred_element_type=jnp.float32),
            jnp.dot(gathered, key_weight, preferred_element_type=jnp.float32),
            jnp.dot(gathered, value_weight, preferred_element_type=jnp.float32),
        ],
        axis=1,
    )
    token_pos = context_index * local_rows + jnp.arange(local_rows, dtype=jnp.int32)
    positions = token_pos.astype(jnp.float32)
    queries = rotate(
        projected[:, :query_width].reshape(local_rows, heads_here, HD), positions
    ).astype(jnp.bfloat16)
    keys = (
        rotate(
            projected[:, query_width : query_width + key_width].reshape(local_rows, kv_here, HD),
            positions,
        )
        .astype(jnp.bfloat16)
        .reshape(local_rows, key_width)
    )
    values = projected[:, query_width + key_width :].astype(jnp.bfloat16)
    groups = []
    for kv_slot in range(kv_here):
        chosen = queries[:, kv_slot * group : (kv_slot + 1) * group].reshape(local_rows * group, HD)
        groups.append(
            (chosen, jnp.repeat(token_pos, group), kv_slot, math.gcd(local_rows * group, 512))
        )
    results = attend(groups, keys, values)
    pieces = [outcome.astype(jnp.bfloat16).reshape(local_rows, group * HD) for outcome in results]
    return jnp.concatenate(pieces, axis=1)


def solution(mesh):
    in_specs = (P(("ctx", "tp"), None), P(None, "tp"), P(None, "tp"), P(None, "tp"))
    out_specs = P("ctx", "tp")
    return jax.shard_map(local, mesh=mesh, in_specs=in_specs, out_specs=out_specs, check_vma=False)
```

profile of v0, /device:TPU:25, one launch (start us, length us, event | category | flops | bytes accessed | tf_op | source)
XLA Modules:
  0.0 219.5 jit_solution(12466268835597819170)
XLA Ops:
  7.6 23.6 %all-gather.4.cloned.1.call-done = bf16[128,4096]{1,0:T(8,128)(2,1)} async-done(((bf16[64,4096]{1,0:T(8,128)(2,1)}), bf16[128,4096]{1,0:T(8,128)(2,1)}) %all-gather.4.cloned.1.call-update) | async-done | bytes 1048592 | tf_op jit(solution)/shard_map/all_gather | solution.py:127
  31.2 3.3 %fusion.78 = f32[128,512]{1,0:T(8,128)S(1)} fusion(bf16[128,4096]{1,0:T(8,128)(2,1)} %all-gather.4.cloned.1.call-done, bf16[4096,512]{1,0:T(8,128)(2,1)} %param.22), kind=kOutput, calls=%fused_computation.123 | convolution fusion | flops 536870912 | bytes 5505024 | tf_op jit(solution)/shard_map/dot_general | solution.py:131
  36.0 3.6 %convolution_convert_fusion = bf16[128,512]{1,0:T(8,128)(2,1)} fusion(bf16[128,4096]{1,0:T(8,128)(2,1)S(1)} %copy-done, bf16[4096,512]{1,0:T(8,128)(2,1)} %param.23), kind=kOutput, calls=%fused_computation.93 | convolution fusion | flops 536936448 | bytes 5373952 | tf_op jit(solution)/shard_map/dot_general | solution.py:132
  40.3 8.2 %convolution_bitcast_fusion = f32[16,8,16,128]{3,1,2,0:T(8,128)S(1)} fusion(bf16[128,4096]{1,0:T(8,128)(2,1)S(1)} %copy-done, bf16[4096,2048]{1,0:T(8,128)(2,1)} %param.21), kind=kOutput, calls=%fused_computation.92 | convolution fusion | flops 2147483648 | bytes 18874368 | tf_op jit(solution)/shard_map/dot_general | solution.py:130
  49.3 1.3 fusion.73
  50.6 25.6 %all-gather.6.cloned.1.call-done = bf16[2048,512]{0,1:T(8,128)(2,1)} async-done(((bf16[128,512]{0,1:T(8,128)(2,1)}), bf16[2048,512]{0,1:T(8,128)(2,1)}) %all-gather.6.cloned.1.call-update) | async-done | bytes 2097168 | tf_op jit(solution)/shard_map/all_gather | solution.py:64
  76.1 2.7 %fusion.77 = (bf16[2048,1,128]{0,2,1:T(8,128)(2,1)S(1)}, bf16[2048,1,128]{0,2,1:T(8,128)(2,1)}, bf16[2048,1,128]{0,2,1:T(8,128)(2,1)}, bf16[2048,1,128]{0,2,1:T(8,128)(2,1)}) fusion(bf16[2048,4,128]{0,2,1:T(8,128)(2,1)} %bitcast.80), kind=kLoop, calls=%fused_computation.122 | loop fusion | bytes 4194304 | tf_op jit(solution)/shard_map/jit(dynamic_index_in_dim)/dynamic_slice | solution.py:70
  79.9 39.1 %all-gather.8.cloned.1.call-done = bf16[2048,512]{1,0:T(8,128)(2,1)} async-done(((bf16[128,512]{1,0:T(8,128)(2,1)}), bf16[2048,512]{1,0:T(8,128)(2,1)}) %all-gather.8.cloned.1.call-update) | async-done | bytes 2097168 | tf_op jit(solution)/shard_map/all_gather | solution.py:65
  119.0 2.5 %reshape.177 = bf16[2048,4,128]{2,1,0:T(4,128)(2,1)S(1)} reshape(bf16[2048,512]{1,0:T(8,128)(2,1)} %all-gather.8.cloned.1.call-done) | data formatting | bytes 4194304 | tf_op jit(solution)/shard_map/reshape | solution.py:74
  121.5 4.0 %fusion.76 = (bf16[2048,1,128]{2,1,0:T(2,128)(2,1)S(1)}, bf16[2048,1,128]{2,1,0:T(2,128)(2,1)}, bf16[2048,1,128]{2,1,0:T(2,128)(2,1)}, bf16[2048,1,128]{2,1,0:T(2,128)(2,1)S(1)}) fusion(bf16[2048,4,128]{2,1,0:T(4,128)(2,1)S(1)} %reshape.177), kind=kLoop, calls=%fused_computation.121 | loop fusion | bytes 4194304 | tf_op jit(solution)/shard_map/jit(dynamic_index_in_dim)/dynamic_slice | solution.py:73
  126.5 22.5 %while.96 = (s32[]{:T(128)}, f32[512]{0:T(512)S(1)}, f32[512]{0:T(512)S(1)}, f32[512,128]{1,0:T(8,128)S(1)}, s32[4]{0:T(128)S(1)}, /*index=5*/s32[]{:T(128)}, bf...) while((s32[]{:T(128)}, f32[512]{0:T(512)S(1)}, ...), condition=%wide.region_6.7_spmd.clone, body=%wide.region_1.0_spmd.clone.sunk | while | flops 137496064 | bytes 4122387 | solution.py:100
  128.3 3.8 %conditional.12 = ((f32[512]{0:T(512)S(1)}, f32[512]{0:T(512)S(1)}, f32[512,128]{1,0:T(8,128)S(1)})) conditional(s32[]{:T(128)} %convert_element_type.119, (f32[512]{0:T(512)S(1)}, f32[512]{0:T(512)S(1)}, f32[512,128]{1,0:T(8,128)S(1)}) %tuple.163, (s32[]{:T(128)}, s32[512]{0:T(512)S(1)}, s32[128]{0:T(128)S(1)}, bf16[4,512,128]{2,1,0:T(8,128)(2,1)}, ...), branch_computations={%region_2.2_spmd, %region_3.5_spmd} | conditional | flops 137496064 | bytes 4120100 | solution.py:90
  129.1 1.3 fusion.9
  130.7 1.4 convolution_add_fusion
  133.9 3.8 %conditional.12 = ((f32[512]{0:T(512)S(1)}, f32[512]{0:T(512)S(1)}, f32[512,128]{1,0:T(8,128)S(1)})) conditional(s32[]{:T(128)} %convert_element_type.119, (f32[512]{0:T(512)S(1)}, f32[512]{0:T(512)S(1)}, f32[512,128]{1,0:T(8,128)S(1)}) %tuple.163, (s32[]{:T(128)}, s32[512]{0:T(512)S(1)}, s32[128]{0:T(128)S(1)}, bf16[4,512,128]{2,1,0:T(8,128)(2,1)}, ...), branch_computations={%region_2.2_spmd, %region_3.5_spmd} | conditional | flops 137496064 | bytes 4120100 | solution.py:90
  134.7 1.3 fusion.9
  136.3 1.4 convolution_add_fusion
  139.5 3.8 %conditional.12 = ((f32[512]{0:T(512)S(1)}, f32[512]{0:T(512)S(1)}, f32[512,128]{1,0:T(8,128)S(1)})) conditional(s32[]{:T(128)} %convert_element_type.119, (f32[512]{0:T(512)S(1)}, f32[512]{0:T(512)S(1)}, f32[512,128]{1,0:T(8,128)S(1)}) %tuple.163, (s32[]{:T(128)}, s32[512]{0:T(512)S(1)}, s32[128]{0:T(128)S(1)}, bf16[4,512,128]{2,1,0:T(8,128)(2,1)}, ...), branch_computations={%region_2.2_spmd, %region_3.5_spmd} | conditional | flops 137496064 | bytes 4120100 | solution.py:90
  140.3 1.3 fusion.9
  141.9 1.4 convolution_add_fusion
  145.2 3.8 %conditional.12 = ((f32[512]{0:T(512)S(1)}, f32[512]{0:T(512)S(1)}, f32[512,128]{1,0:T(8,128)S(1)})) conditional(s32[]{:T(128)} %convert_element_type.119, (f32[512]{0:T(512)S(1)}, f32[512]{0:T(512)S(1)}, f32[512,128]{1,0:T(8,128)S(1)}) %tuple.163, (s32[]{:T(128)}, s32[512]{0:T(512)S(1)}, s32[128]{0:T(128)S(1)}, bf16[4,512,128]{2,1,0:T(8,128)(2,1)}, ...), branch_computations={%region_2.2_spmd, %region_3.5_spmd} | conditional | flops 137496064 | bytes 4120100 | solution.py:90
  145.9 1.3 fusion.9
  147.5 1.4 convolution_add_fusion
  151.2 23.1 %while.97 = (s32[]{:T(128)}, f32[512]{0:T(512)S(1)}, f32[512]{0:T(512)S(1)}, f32[512,128]{1,0:T(8,128)S(1)}, s32[4]{0:T(128)S(1)}, /*index=5*/s32[]{:T(128)}, bf...) while((s32[]{:T(128)}, f32[512]{0:T(512)S(1)}, ...), condition=%wide.region_12.13_spmd.clone, body=%wide.region_7.12_spmd.clone.sunk | while | flops 137496064 | bytes 4122387 | solution.py:100
  153.1 3.9 %conditional.13 = ((f32[512]{0:T(512)S(1)}, f32[512]{0:T(512)S(1)}, f32[512,128]{1,0:T(8,128)S(1)})) conditional(s32[]{:T(128)} %convert_element_type.120, (f32[512]{0:T(512)S(1)}, f32[512]{0:T(512)S(1)}, f32[512,128]{1,0:T(8,128)S(1)}) %tuple.166, (s32[]{:T(128)}, s32[512]{0:T(512)S(1)}, s32[128]{0:T(128)S(1)}, bf16[4,512,128]{2,1,0:T(8,128)(2,1)}, ...), branch_computations={%region_8.8_spmd, %region_9.11_spmd} | conditional | flops 137496064 | bytes 4120100 | solution.py:90
  153.9 1.3 fusion.25
  155.5 1.4 convolution_add_fusion.1
  158.9 3.9 %conditional.13 = ((f32[512]{0:T(512)S(1)}, f32[512]{0:T(512)S(1)}, f32[512,128]{1,0:T(8,128)S(1)})) conditional(s32[]{:T(128)} %convert_element_type.120, (f32[512]{0:T(512)S(1)}, f32[512]{0:T(512)S(1)}, f32[512,128]{1,0:T(8,128)S(1)}) %tuple.166, (s32[]{:T(128)}, s32[512]{0:T(512)S(1)}, s32[128]{0:T(128)S(1)}, bf16[4,512,128]{2,1,0:T(8,128)(2,1)}, ...), branch_computations={%region_8.8_spmd, %region_9.11_spmd} | conditional | flops 137496064 | bytes 4120100 | solution.py:90
  159.7 1.3 fusion.25
  161.3 1.4 convolution_add_fusion.1
  164.7 3.9 %conditional.13 = ((f32[512]{0:T(512)S(1)}, f32[512]{0:T(512)S(1)}, f32[512,128]{1,0:T(8,128)S(1)})) conditional(s32[]{:T(128)} %convert_element_type.120, (f32[512]{0:T(512)S(1)}, f32[512]{0:T(512)S(1)}, f32[512,128]{1,0:T(8,128)S(1)}) %tuple.166, (s32[]{:T(128)}, s32[512]{0:T(512)S(1)}, s32[128]{0:T(128)S(1)}, bf16[4,512,128]{2,1,0:T(8,128)(2,1)}, ...), branch_computations={%region_8.8_spmd, %region_9.11_spmd} | conditional | flops 137496064 | bytes 4120100 | solution.py:90
  165.5 1.3 fusion.25
  167.1 1.4 convolution_add_fusion.1
  170.4 3.9 %conditional.13 = ((f32[512]{0:T(512)S(1)}, f32[512]{0:T(512)S(1)}, f32[512,128]{1,0:T(8,128)S(1)})) conditional(s32[]{:T(128)} %convert_element_type.120, (f32[512]{0:T(512)S(1)}, f32[512]{0:T(512)S(1)}, f32[512,128]{1,0:T(8,128)S(1)}) %tuple.166, (s32[]{:T(128)}, s32[512]{0:T(512)S(1)}, s32[128]{0:T(128)S(1)}, bf16[4,512,128]{2,1,0:T(8,128)(2,1)}, ...), branch_computations={%region_8.8_spmd, %region_9.11_spmd} | conditional | flops 137496064 | bytes 4120100 | solution.py:90
  171.3 1.3 fusion.25
  172.9 1.4 convolution_add_fusion.1
  175.7 19.9 %while.98 = (s32[]{:T(128)}, f32[512]{0:T(512)S(1)}, f32[512]{0:T(512)S(1)}, f32[512,128]{1,0:T(8,128)S(1)}, s32[4]{0:T(128)S(1)}, /*index=5*/s32[]{:T(128)}, bf...) while((s32[]{:T(128)}, f32[512]{0:T(512)S(1)}, ...), condition=%wide.region_18.19_spmd.clone, body=%wide.region_13.18_spmd.clone.sunk | while | flops 137496064 | bytes 4121879 | solution.py:100
  177.8 2.9 %conditional.14 = ((f32[512]{0:T(512)S(1)}, f32[512]{0:T(512)S(1)}, f32[512,128]{1,0:T(8,128)S(1)})) conditional(s32[]{:T(128)} %convert_element_type.121, (f32[512]{0:T(512)S(1)}, f32[512]{0:T(512)S(1)}, f32[512,128]{1,0:T(8,128)S(1)}) %tuple.169, (s32[]{:T(128)}, s32[512]{0:T(512)S(1)}, s32[128]{0:T(128)S(1)}, bf16[4,512,128]{2,1,0:T(8,128)(2,1)}, ...), branch_computations={%region_14.14_spmd, %region_15.17_spmd} | conditional | flops 137496064 | bytes 4119592 | solution.py:90
  178.7 1.2 fusion.41
  182.7 2.9 %conditional.14 = ((f32[512]{0:T(512)S(1)}, f32[512]{0:T(512)S(1)}, f32[512,128]{1,0:T(8,128)S(1)})) conditional(s32[]{:T(128)} %convert_element_type.121, (f32[512]{0:T(512)S(1)}, f32[512]{0:T(512)S(1)}, f32[512,128]{1,0:T(8,128)S(1)}) %tuple.169, (s32[]{:T(128)}, s32[512]{0:T(512)S(1)}, s32[128]{0:T(128)S(1)}, bf16[4,512,128]{2,1,0:T(8,128)(2,1)}, ...), branch_computations={%region_14.14_spmd, %region_15.17_spmd} | conditional | flops 137496064 | bytes 4119592 | solution.py:90
  187.7 2.9 %conditional.14 = ((f32[512]{0:T(512)S(1)}, f32[512]{0:T(512)S(1)}, f32[512,128]{1,0:T(8,128)S(1)})) conditional(s32[]{:T(128)} %convert_element_type.121, (f32[512]{0:T(512)S(1)}, f32[512]{0:T(512)S(1)}, f32[512,128]{1,0:T(8,128)S(1)}) %tuple.169, (s32[]{:T(128)}, s32[512]{0:T(512)S(1)}, s32[128]{0:T(128)S(1)}, bf16[4,512,128]{2,1,0:T(8,128)(2,1)}, ...), branch_computations={%region_14.14_spmd, %region_15.17_spmd} | conditional | flops 137496064 | bytes 4119592 | solution.py:90
  188.6 1.2 fusion.41
  192.7 2.9 %conditional.14 = ((f32[512]{0:T(512)S(1)}, f32[512]{0:T(512)S(1)}, f32[512,128]{1,0:T(8,128)S(1)})) conditional(s32[]{:T(128)} %convert_element_type.121, (f32[512]{0:T(512)S(1)}, f32[512]{0:T(512)S(1)}, f32[512,128]{1,0:T(8,128)S(1)}) %tuple.169, (s32[]{:T(128)}, s32[512]{0:T(512)S(1)}, s32[128]{0:T(128)S(1)}, bf16[4,512,128]{2,1,0:T(8,128)(2,1)}, ...), branch_computations={%region_14.14_spmd, %region_15.17_spmd} | conditional | flops 137496064 | bytes 4119592 | solution.py:90
  196.3 15.6 %while.99 = (s32[]{:T(128)}, f32[512]{0:T(512)S(1)}, f32[512]{0:T(512)S(1)}, f32[512,128]{1,0:T(8,128)S(1)}, s32[4]{0:T(128)S(1)}, /*index=5*/s32[]{:T(128)}, bf...) while((s32[]{:T(128)}, f32[512]{0:T(512)S(1)}, ...), condition=%wide.region_24.25_spmd.clone, body=%wide.region_19.24_spmd.clone.sunk | while | flops 137496064 | bytes 4121371 | solution.py:100
  198.2 2.0 conditional.15
  202.1 2.0 conditional.15
  206.0 2.0 conditional.15
  209.9 2.0 conditional.15
  (216 shorter events, 46.2 us)
Async XLA Ops:
  6.5 24.7 %all-gather.4.cloned.1.call-start = ((), (), s32[]{:S(2)}) async-start(), calls=%async_computation | async-start | bytes 1572864 | tf_op jit(solution)/shard_map/all_gather | solution.py:127
  7.3 68.9 %all-gather.6.cloned.1.call-start = ((), (), s32[]{:S(2)}) async-start(), calls=%async_computation.1 | async-start | bytes 2228224 | tf_op jit(solution)/shard_map/all_gather | solution.py:64
  31.2 4.8 %copy-start = (bf16[128,4096]{1,0:T(8,128)(2,1)S(1)}, bf16[128,4096]{1,0:T(8,128)(2,1)}, u32[]{:S(2)}) copy-start(bf16[128,4096]{1,0:T(8,128)(2,1)} %all-gather.4.cloned.1.call-done) | copy-start | bytes 3145732
  35.9 83.1 %all-gather.8.cloned.1.call-start = ((), (), s32[]{:S(2)}) async-start(), calls=%async_computation.2 | async-start | bytes 2228224 | tf_op jit(solution)/shard_map/all_gather | solution.py:65
  126.5 22.7 %copy-start.5 = (bf16[2048,1,128]{0,2,1:T(8,128)(2,1)S(1)}, bf16[2048,1,128]{0,2,1:T(8,128)(2,1)}, u32[]{:S(2)}) copy-start(bf16[2048,1,128]{0,2,1:T(8,128)(2,1)} %get-tuple-element.984) | copy-start | bytes 1572868
  126.5 23.7 %copy-start.2 = (bf16[2048,1,128]{2,1,0:T(2,128)(2,1)S(1)}, bf16[2048,1,128]{2,1,0:T(2,128)(2,1)}, u32[]{:S(2)}) copy-start(bf16[2048,1,128]{2,1,0:T(2,128)(2,1)} %get-tuple-element.979) | copy-start | bytes 1572868
  151.2 23.4 %copy-start.4 = (bf16[2048,1,128]{0,2,1:T(8,128)(2,1)S(1)}, bf16[2048,1,128]{0,2,1:T(8,128)(2,1)}, u32[]{:S(2)}) copy-start(bf16[2048,1,128]{0,2,1:T(8,128)(2,1)} %get-tuple-element.983) | copy-start | bytes 1572868
  151.2 24.4 %copy-start.1 = (bf16[2048,1,128]{2,1,0:T(2,128)(2,1)S(1)}, bf16[2048,1,128]{2,1,0:T(2,128)(2,1)}, u32[]{:S(2)}) copy-start(bf16[2048,1,128]{2,1,0:T(2,128)(2,1)} %get-tuple-element.978) | copy-start | bytes 1572868
  175.7 20.1 %copy-start.3 = (bf16[2048,1,128]{0,2,1:T(8,128)(2,1)S(1)}, bf16[2048,1,128]{0,2,1:T(8,128)(2,1)}, u32[]{:S(2)}) copy-start(bf16[2048,1,128]{0,2,1:T(8,128)(2,1)} %get-tuple-element.982) | copy-start | bytes 1572868
Sparse Core Ops, SparseCore 0:
  8.9 22.2 all-gather.3
  36.0 40.0 all-gather.5
  78.3 40.6 all-gather.7
where the time goes:
time: 221 us; the launch traced here: 219 us
  waiting for transfers between devices  89 us (40%)
  matrix products  47.3 us (21%)
  local copies, waits for them, and re-layouts  28.9 us (13%)
  loops' own time  21.6 us (10%)
  other arithmetic  19.1 us (9%)
  between operations  13.5 us (6%)
    all_gather x1, waiting for transfers between devices, attend(): value_piece = lax.all_gather(values, 'ctx', axis=0, tiled=True)  39.1 us
    all_gather x1, waiting for transfers between devices, attend(): key_piece = lax.all_gather(keys, 'ctx', axis=0, tiled=True)  25.6 us
    all_gather x1, waiting for transfers between devices, local(): gathered = lax.all_gather(activations, 'tp', axis=0, tiled=True)  23.6 us
    another operation x4, loops' own time, per_query(): lax.scan(per_key, (row_top, totals, accum), (key_blocks, value_blocks, bl...  20.8 us
    dot_general x16, matrix products, block_update(): lax.dot_general(query_block, key_block, (((1,), (1,)), ((), ())), preferr...  16.5 us
    dot_general x16, matrix products, block_update(): jnp.dot(weights.astype(jnp.bfloat16), value_block, preferred_element_type...  15.7 us
    add x16, other arithmetic, per_key(): key_pos = key_start + jnp.arange(key_step, dtype=jnp.int32)  10.2 us
    dynamic_slice x16, local copies, waits for them, and re-layouts, per_query(): lax.scan(per_key, (row_top, totals, accum), (key_blocks, value_blocks, bl...  9.76 us
  transfers between devices with their start and end apart: 3, of which 3 were waited for; matrix products, arithmetic and copies ran while one was open for 8% of the time, Pallas kernels for 0%

commit v1 on v0

--- a/solution.py
+++ b/solution.py
@@ -7,6 +7,28 @@
 HD = 128
 THETA = 500000.0
 NEGATIVE = -1e30
+
+
+def laid_out(blocks, dim):
+    shape = list(blocks.shape[1:])
+    shape[dim] *= blocks.shape[0]
+    return jnp.moveaxis(blocks, 0, dim).reshape(shape)
+
+
+def ring_gather(array, axis, dim):
+    devices = lax.axis_size(axis)
+    pairs = [(i, (i + 1) % devices) for i in range(devices)]
+    back = [(b, a) for a, b in pairs]
+    lower, upper = ([], [])
+    for step in range(devices - 1):
+        if step % 2 == 0:
+            lower.append(lax.ppermute(lower[-1] if lower else array, axis, pairs))
+        else:
+            upper.append(lax.ppermute(upper[-1] if upper else array, axis, back))
+    tiles = jnp.stack([*lower[::-1], array, *upper])
+    shift = lax.axis_index(axis) - len(lower)
+    tiles = tiles[(jnp.arange(devices) - shift) % devices]
+    return laid_out(tiles, dim)
 
 
 def rotate(heads_in, positions):
@@ -61,7 +83,7 @@
             )
         )
     carry = tuple(carry_start)
-    key_piece = lax.all_gather(keys, "ctx", axis=0, tiled=True)
+    key_piece = ring_gather(keys, "ctx", 0)
     value_piece = lax.all_gather(values, "ctx", axis=0, tiled=True)
     piece_rows = key_piece.shape[0]
     key_step = math.gcd(piece_rows, 512)

time: 221 us -> 207 us (0.937)
  waiting for transfers between devices: 89 us -> 53.5 us
  starting transfers between devices: 0.08 us -> 26.5 us
  matrix products: 47.3 us -> 43.1 us
  local copies, waits for them, and re-layouts: 28.9 us -> 31.3 us
    all_gather x1, waiting for transfers between devices: 39.1 us -> 10.6 us  [attend(): value_piece = lax.all_gather(values, 'ctx', axis=0, tiled=True)]
    ppermute x0 -> x15, starting transfers between devices: none -> 26.4 us  [the longest x8 25.5 us: ring_gather(): lower.append(lax.ppermute(lower[-1] if lower else array, axis, pairs))]
    all_gather x1 -> x0, waiting for transfers between devices: 25.6 us -> none  [attend(): key_piece = lax.all_gather(keys, 'ctx', axis=0, tiled=True)]
    ppermute x0 -> x15, waiting for transfers between devices: none -> 18.6 us  [the longest x7 13.7 us: ring_gather(): upper.append(lax.ppermute(upper[-1] if upper else array, axis, back))]
    dot_general x16, matrix products: 15.7 us -> 8.29 us  [block_update(): jnp.dot(weights.astype(jnp.bfloat16), value_block, preferred_element_type...]
    dot_general x16, matrix products: 16.5 us -> 19.9 us  [block_update(): lax.dot_general(query_block, key_block, (((1,), (1,)), ((), ())), preferr...]
    another operation x0 -> x2, local copies, waits for them, and re-layouts: none -> 2.55 us  [the longest x1 2.55 us: attend(): key_piece.reshape(piece_rows, -1, HD)]
    unnamed x21 -> x43, local copies, waits for them, and re-layouts: 5.44 us -> 4.15 us
  transfers between devices with their start and end apart: 3 -> 17, of which waited for: 3 -> 12; matrix products, arithmetic and copies ran while one was open for 8% -> 13% of each run, Pallas kernels for 0% -> 0%
where the time goes in v1:
time: 207 us; the launch traced here: 206 us
  waiting for transfers between devices  53.5 us (26%)
  matrix products  43.1 us (21%)
  local copies, waits for them, and re-layouts  31.3 us (15%)
  starting transfers between devices  26.5 us (13%)
  loops' own time  19.7 us (10%)
  other arithmetic  18 us (9%)
  between operations  14 us (7%)
    ppermute x8, starting transfers between devices, ring_gather(): lower.append(lax.ppermute(lower[-1] if lower else array, axis, pairs))  25.5 us
    all_gather x1, waiting for transfers between devices, local(): gathered = lax.all_gather(activations, 'tp', axis=0, tiled=True)  23.6 us
    dot_general x16, matrix products, block_update(): lax.dot_general(query_block, key_block, (((1,), (1,)), ((), ())), preferr...  19.9 us
    another operation x4, loops' own time, per_query(): lax.scan(per_key, (row_top, totals, accum), (key_blocks, value_blocks, bl...  18.8 us
    ppermute x7, waiting for transfers between devices, ring_gather(): upper.append(lax.ppermute(upper[-1] if upper else array, axis, back))  13.7 us
    all_gather x1, waiting for transfers between devices, attend(): value_piece = lax.all_gather(values, 'ctx', axis=0, tiled=True)  10.6 us
    dynamic_slice x16, local copies, waits for them, and re-layouts, per_query(): lax.scan(per_key, (row_top, totals, accum), (key_blocks, value_blocks, bl...  9.26 us
    add x16, other arithmetic, per_key(): key_pos = key_start + jnp.arange(key_step, dtype=jnp.int32)  9.23 us
  transfers between devices with their start and end apart: 17, of which 12 were waited for; matrix products, arithmetic and copies ran while one was open for 13% of the time, Pallas kernels for 0%

profile of v1, /device:TPU:25, one launch (start us, length us, event | category | flops | bytes accessed | tf_op | source)
XLA Modules:
  0.0 206.0 jit_solution(9543712272757769611)
XLA Ops:
  7.6 23.6 %all-gather.3.cloned.1.call-done = bf16[128,4096]{1,0:T(8,128)(2,1)} async-done(((bf16[64,4096]{1,0:T(8,128)(2,1)}), bf16[128,4096]{1,0:T(8,128)(2,1)}) %all-gather.3.cloned.1.call-update) | async-done | bytes 1048592 | tf_op jit(solution)/shard_map/all_gather | solution.py:149
  31.2 3.2 %fusion.80 = f32[128,512]{1,0:T(8,128)S(1)} fusion(bf16[128,4096]{1,0:T(8,128)(2,1)} %all-gather.3.cloned.1.call-done, bf16[4096,512]{1,0:T(8,128)(2,1)} %param.22), kind=kOutput, calls=%fused_computation.148 | convolution fusion | flops 536870912 | bytes 5505024 | tf_op jit(solution)/shard_map/dot_general | solution.py:153
  35.1 1.8 collective-permute-start
  36.9 1.9 collective-permute-done
  38.8 2.4 %collective-permute-start.1 = (bf16[128,512]{1,0:T(8,128)(2,1)S(1)}, bf16[128,512]{1,0:T(8,128)(2,1)S(1)}, u32[]{:S(2)}, u32[]{:S(2)}) collective-permute-start(bf16[128,512]{1,0:T(8,128)(2,1)S(1)} %collective-permute-done), channel_id=1, source_target_pairs={{0,2},{2,4},{4,6},{6,8},{8,10},{10,12},{12,14},{14,16},{16,18},{18... | collective-permute-start | bytes 393224 | tf_op jit(solution)/shard_map/ppermute | solution.py:25
  41.3 1.9 collective-permute-done.1
  43.2 2.4 %collective-permute-start.2 = (bf16[128,512]{1,0:T(8,128)(2,1)S(1)}, bf16[128,512]{1,0:T(8,128)(2,1)S(1)}, u32[]{:S(2)}, u32[]{:S(2)}) collective-permute-start(bf16[128,512]{1,0:T(8,128)(2,1)S(1)} %collective-permute-done.1), channel_id=1, source_target_pairs={{0,2},{2,4},{4,6},{6,8},{8,10},{10,12},{12,14},{14,16},{16,18},{18... | collective-permute-start | bytes 393224 | tf_op jit(solution)/shard_map/ppermute | solution.py:25
  45.7 1.4 collective-permute-done.8
  47.6 2.4 %collective-permute-start.3 = (bf16[128,512]{1,0:T(8,128)(2,1)S(1)}, bf16[128,512]{1,0:T(8,128)(2,1)S(1)}, u32[]{:S(2)}, u32[]{:S(2)}) collective-permute-start(bf16[128,512]{1,0:T(8,128)(2,1)S(1)} %collective-permute-done.2), channel_id=1, source_target_pairs={{0,2},{2,4},{4,6},{6,8},{8,10},{10,12},{12,14},{14,16},{16,18},{18... | collective-permute-start | bytes 393224 | tf_op jit(solution)/shard_map/ppermute | solution.py:25
  50.7 1.8 collective-permute-done.9
  52.7 1.9 collective-permute-start.4
  54.7 3.2 %collective-permute-done.10 = bf16[128,512]{1,0:T(8,128)(2,1)S(1)} collective-permute-done((bf16[128,512]{1,0:T(8,128)(2,1)S(1)}, bf16[128,512]{1,0:T(8,128)(2,1)S(1)}, u32[]{:S(2)}, u32[]{:S(2)}) %collective-permute-start.10) | collective-permute-done | bytes 131104 | tf_op jit(solution)/shard_map/ppermute | solution.py:27
  58.1 3.7 %collective-permute-start.5 = (bf16[128,512]{1,0:T(8,128)(2,1)S(1)}, bf16[128,512]{1,0:T(8,128)(2,1)S(1)}, u32[]{:S(2)}, u32[]{:S(2)}) collective-permute-start(bf16[128,512]{1,0:T(8,128)(2,1)S(1)} %collective-permute-done.4), channel_id=1, source_target_pairs={{0,2},{2,4},{4,6},{6,8},{8,10},{10,12},{12,14},{14,16},{16,18},{18... | collective-permute-start | bytes 393224 | tf_op jit(solution)/shard_map/ppermute | solution.py:25
  61.9 3.6 %convolution_convert_fusion = bf16[128,512]{1,0:T(8,128)(2,1)} fusion(bf16[128,4096]{1,0:T(8,128)(2,1)S(1)} %copy-done, bf16[4096,512]{1,0:T(8,128)(2,1)} %param.23), kind=kOutput, calls=%fused_computation.94 | convolution fusion | flops 536936448 | bytes 5373952 | tf_op jit(solution)/shard_map/dot_general | solution.py:154
  66.4 5.5 %collective-permute-start.6 = (bf16[128,512]{1,0:T(8,128)(2,1)S(1)}, bf16[128,512]{1,0:T(8,128)(2,1)S(1)}, u32[]{:S(2)}, u32[]{:S(2)}) collective-permute-start(bf16[128,512]{1,0:T(8,128)(2,1)S(1)} %collective-permute-done.5), channel_id=1, source_target_pairs={{0,2},{2,4},{4,6},{6,8},{8,10},{10,12},{12,14},{14,16},{16,18},{18... | collective-permute-start | bytes 393224 | tf_op jit(solution)/shard_map/ppermute | solution.py:25
  71.9 8.1 %convolution_bitcast_fusion = f32[16,8,16,128]{3,1,2,0:T(8,128)S(1)} fusion(bf16[128,4096]{1,0:T(8,128)(2,1)S(1)} %copy-done, bf16[4096,2048]{1,0:T(8,128)(2,1)} %param.21), kind=kOutput, calls=%fused_computation.93 | convolution fusion | flops 2147483648 | bytes 18874368 | tf_op jit(solution)/shard_map/dot_general | solution.py:152
  80.3 5.2 %collective-permute-start.7 = (bf16[128,512]{1,0:T(8,128)(2,1)S(1)}, bf16[128,512]{1,0:T(8,128)(2,1)S(1)}, u32[]{:S(2)}, u32[]{:S(2)}) collective-permute-start(bf16[128,512]{1,0:T(8,128)(2,1)S(1)} %collective-permute-done.6), channel_id=1, source_target_pairs={{0,2},{2,4},{4,6},{6,8},{8,10},{10,12},{12,14},{14,16},{16,18},{18... | collective-permute-start | bytes 393224 | tf_op jit(solution)/shard_map/ppermute | solution.py:25
  88.6 6.2 %collective-permute-done.14 = bf16[128,512]{1,0:T(8,128)(2,1)S(1)} collective-permute-done((bf16[128,512]{1,0:T(8,128)(2,1)S(1)}, bf16[128,512]{1,0:T(8,128)(2,1)S(1)}, u32[]{:S(2)}, u32[]{:S(2)}) %collective-permute-start.14) | collective-permute-done | bytes 131104 | tf_op jit(solution)/shard_map/ppermute | solution.py:27
  94.8 2.0 gather_fusion
  96.9 2.5 %reshape.246 = bf16[2048,4,128]{2,1,0:T(4,128)(2,1)S(1)} reshape(bf16[16,128,512]{2,1,0:T(8,128)(2,1)} %gather_fusion) | data formatting | bytes 4194304 | tf_op jit(solution)/shard_map/reshape;reshape | solution.py:93
  99.4 3.1 %fusion.79 = (bf16[2048,1,128]{2,1,0:T(2,128)(2,1)S(1)}, bf16[2048,1,128]{2,1,0:T(2,128)(2,1)S(1)}, bf16[2048,1,128]{2,1,0:T(2,128)(2,1)S(1)}, bf16[2048,1,128]{2,1,0:T(2,128)(2,1)S(1)}) fusion(bf16[2048,4,128]{2,1,0:T(4,128)(2,1)S(1)} %reshape.246), kind=kLoop, calls=%fused_computation.147 | loop fusion | bytes 4194304 | tf_op jit(solution)/shard_map/jit(dynamic_index_in_dim)/dynamic_slice | solution.py:92
  105.9 10.6 %all-gather.5.cloned.1.call-done = bf16[2048,512]{1,0:T(8,128)(2,1)} async-done(((bf16[128,512]{1,0:T(8,128)(2,1)}), bf16[2048,512]{1,0:T(8,128)(2,1)}) %all-gather.5.cloned.1.call-update) | async-done | bytes 2097168 | tf_op jit(solution)/shard_map/all_gather | solution.py:87
  116.6 2.5 %reshape.230 = bf16[2048,4,128]{2,1,0:T(4,128)(2,1)S(1)} reshape(bf16[2048,512]{1,0:T(8,128)(2,1)} %all-gather.5.cloned.1.call-done) | data formatting | bytes 4194304 | tf_op jit(solution)/shard_map/reshape | solution.py:96
  119.1 4.0 %fusion.78 = (bf16[2048,1,128]{2,1,0:T(2,128)(2,1)S(1)}, bf16[2048,1,128]{2,1,0:T(2,128)(2,1)}, bf16[2048,1,128]{2,1,0:T(2,128)(2,1)}, bf16[2048,1,128]{2,1,0:T(2,128)(2,1)S(1)}) fusion(bf16[2048,4,128]{2,1,0:T(4,128)(2,1)S(1)} %reshape.230), kind=kLoop, calls=%fused_computation.146 | loop fusion | bytes 4194304 | tf_op jit(solution)/shard_map/jit(dynamic_index_in_dim)/dynamic_slice | solution.py:95
  123.3 18.2 %while.96 = (s32[]{:T(128)}, f32[512]{0:T(512)S(1)}, f32[512]{0:T(512)S(1)}, f32[512,128]{1,0:T(8,128)S(1)}, s32[4]{0:T(128)S(1)}, /*index=5*/s32[]{:T(128)}, bf...) while((s32[]{:T(128)}, f32[512]{0:T(512)S(1)}, ...), condition=%wide.region_6.7_spmd.clone, body=%wide.region_1.6_spmd.clone.sunk | while | flops 137496064 | bytes 4121887 | solution.py:122
  125.0 2.9 %conditional.12 = ((f32[512]{0:T(512)S(1)}, f32[512]{0:T(512)S(1)}, f32[512,128]{1,0:T(8,128)S(1)})) conditional(s32[]{:T(128)} %convert_element_type.134, (f32[512]{0:T(512)S(1)}, f32[512]{0:T(512)S(1)}, f32[512,128]{1,0:T(8,128)S(1)}) %tuple.167, (s32[]{:T(128)}, s32[512]{0:T(512)S(1)}, s32[128]{0:T(128)S(1)}, bf16[4,512,128]{2,1,0:T(8,128)(2,1)}, ...), branch_computations={%region_2.2_spmd, %region_3.5_spmd} | conditional | flops 137496064 | bytes 4119592 | solution.py:112
  125.7 1.3 fusion.9
  129.5 2.9 %conditional.12 = ((f32[512]{0:T(512)S(1)}, f32[512]{0:T(512)S(1)}, f32[512,128]{1,0:T(8,128)S(1)})) conditional(s32[]{:T(128)} %convert_element_type.134, (f32[512]{0:T(512)S(1)}, f32[512]{0:T(512)S(1)}, f32[512,128]{1,0:T(8,128)S(1)}) %tuple.167, (s32[]{:T(128)}, s32[512]{0:T(512)S(1)}, s32[128]{0:T(128)S(1)}, bf16[4,512,128]{2,1,0:T(8,128)(2,1)}, ...), branch_computations={%region_2.2_spmd, %region_3.5_spmd} | conditional | flops 137496064 | bytes 4119592 | solution.py:112
  130.3 1.3 fusion.9
  134.1 2.9 %conditional.12 = ((f32[512]{0:T(512)S(1)}, f32[512]{0:T(512)S(1)}, f32[512,128]{1,0:T(8,128)S(1)})) conditional(s32[]{:T(128)} %convert_element_type.134, (f32[512]{0:T(512)S(1)}, f32[512]{0:T(512)S(1)}, f32[512,128]{1,0:T(8,128)S(1)}) %tuple.167, (s32[]{:T(128)}, s32[512]{0:T(512)S(1)}, s32[128]{0:T(128)S(1)}, bf16[4,512,128]{2,1,0:T(8,128)(2,1)}, ...), branch_computations={%region_2.2_spmd, %region_3.5_spmd} | conditional | flops 137496064 | bytes 4119592 | solution.py:112
  134.9 1.3 fusion.9
  138.7 2.9 %conditional.12 = ((f32[512]{0:T(512)S(1)}, f32[512]{0:T(512)S(1)}, f32[512,128]{1,0:T(8,128)S(1)})) conditional(s32[]{:T(128)} %convert_element_type.134, (f32[512]{0:T(512)S(1)}, f32[512]{0:T(512)S(1)}, f32[512,128]{1,0:T(8,128)S(1)}) %tuple.167, (s32[]{:T(128)}, s32[512]{0:T(512)S(1)}, s32[128]{0:T(128)S(1)}, bf16[4,512,128]{2,1,0:T(8,128)(2,1)}, ...), branch_computations={%region_2.2_spmd, %region_3.5_spmd} | conditional | flops 137496064 | bytes 4119592 | solution.py:112
  139.4 1.3 fusion.9
  141.9 18.3 %while.98 = (s32[]{:T(128)}, f32[512]{0:T(512)S(1)}, f32[512]{0:T(512)S(1)}, f32[512,128]{1,0:T(8,128)S(1)}, s32[4]{0:T(128)S(1)}, /*index=5*/s32[]{:T(128)}, bf...) while((s32[]{:T(128)}, f32[512]{0:T(512)S(1)}, ...), condition=%wide.region_18.19_spmd.clone, body=%wide.region_13.18_spmd.clone.sunk | while | flops 137496064 | bytes 4121887 | solution.py:122
  143.7 2.8 %conditional.14 = ((f32[512]{0:T(512)S(1)}, f32[512]{0:T(512)S(1)}, f32[512,128]{1,0:T(8,128)S(1)})) conditional(s32[]{:T(128)} %convert_element_type.136, (f32[512]{0:T(512)S(1)}, f32[512]{0:T(512)S(1)}, f32[512,128]{1,0:T(8,128)S(1)}) %tuple.173, (s32[]{:T(128)}, s32[512]{0:T(512)S(1)}, s32[128]{0:T(128)S(1)}, bf16[4,512,128]{2,1,0:T(8,128)(2,1)}, ...), branch_computations={%region_14.14_spmd, %region_15.17_spmd} | conditional | flops 137496064 | bytes 4119592 | solution.py:112
  148.2 2.8 %conditional.14 = ((f32[512]{0:T(512)S(1)}, f32[512]{0:T(512)S(1)}, f32[512,128]{1,0:T(8,128)S(1)})) conditional(s32[]{:T(128)} %convert_element_type.136, (f32[512]{0:T(512)S(1)}, f32[512]{0:T(512)S(1)}, f32[512,128]{1,0:T(8,128)S(1)}) %tuple.173, (s32[]{:T(128)}, s32[512]{0:T(512)S(1)}, s32[128]{0:T(128)S(1)}, bf16[4,512,128]{2,1,0:T(8,128)(2,1)}, ...), branch_computations={%region_14.14_spmd, %region_15.17_spmd} | conditional | flops 137496064 | bytes 4119592 | solution.py:112
  152.8 2.8 %conditional.14 = ((f32[512]{0:T(512)S(1)}, f32[512]{0:T(512)S(1)}, f32[512,128]{1,0:T(8,128)S(1)})) conditional(s32[]{:T(128)} %convert_element_type.136, (f32[512]{0:T(512)S(1)}, f32[512]{0:T(512)S(1)}, f32[512,128]{1,0:T(8,128)S(1)}) %tuple.173, (s32[]{:T(128)}, s32[512]{0:T(512)S(1)}, s32[128]{0:T(128)S(1)}, bf16[4,512,128]{2,1,0:T(8,128)(2,1)}, ...), branch_computations={%region_14.14_spmd, %region_15.17_spmd} | conditional | flops 137496064 | bytes 4119592 | solution.py:112
  157.4 2.8 %conditional.14 = ((f32[512]{0:T(512)S(1)}, f32[512]{0:T(512)S(1)}, f32[512,128]{1,0:T(8,128)S(1)})) conditional(s32[]{:T(128)} %convert_element_type.136, (f32[512]{0:T(512)S(1)}, f32[512]{0:T(512)S(1)}, f32[512,128]{1,0:T(8,128)S(1)}) %tuple.173, (s32[]{:T(128)}, s32[512]{0:T(512)S(1)}, s32[128]{0:T(128)S(1)}, bf16[4,512,128]{2,1,0:T(8,128)(2,1)}, ...), branch_computations={%region_14.14_spmd, %region_15.17_spmd} | conditional | flops 137496064 | bytes 4119592 | solution.py:112
  160.6 18.7 %while.97 = (s32[]{:T(128)}, f32[512]{0:T(512)S(1)}, f32[512]{0:T(512)S(1)}, f32[512,128]{1,0:T(8,128)S(1)}, s32[4]{0:T(128)S(1)}, /*index=5*/s32[]{:T(128)}, bf...) while((s32[]{:T(128)}, f32[512]{0:T(512)S(1)}, ...), condition=%wide.region_12.13_spmd.clone, body=%wide.region_7.12_spmd.clone.sunk | while | flops 137496064 | bytes 4121887 | solution.py:122
  162.4 2.9 %conditional.13 = ((f32[512]{0:T(512)S(1)}, f32[512]{0:T(512)S(1)}, f32[512,128]{1,0:T(8,128)S(1)})) conditional(s32[]{:T(128)} %convert_element_type.135, (f32[512]{0:T(512)S(1)}, f32[512]{0:T(512)S(1)}, f32[512,128]{1,0:T(8,128)S(1)}) %tuple.170, (s32[]{:T(128)}, s32[512]{0:T(512)S(1)}, s32[128]{0:T(128)S(1)}, bf16[4,512,128]{2,1,0:T(8,128)(2,1)}, ...), branch_computations={%region_8.8_spmd, %region_9.11_spmd} | conditional | flops 137496064 | bytes 4119592 | solution.py:112
  167.1 2.9 %conditional.13 = ((f32[512]{0:T(512)S(1)}, f32[512]{0:T(512)S(1)}, f32[512,128]{1,0:T(8,128)S(1)})) conditional(s32[]{:T(128)} %convert_element_type.135, (f32[512]{0:T(512)S(1)}, f32[512]{0:T(512)S(1)}, f32[512,128]{1,0:T(8,128)S(1)}) %tuple.170, (s32[]{:T(128)}, s32[512]{0:T(512)S(1)}, s32[128]{0:T(128)S(1)}, bf16[4,512,128]{2,1,0:T(8,128)(2,1)}, ...), branch_computations={%region_8.8_spmd, %region_9.11_spmd} | conditional | flops 137496064 | bytes 4119592 | solution.py:112
  171.8 2.9 %conditional.13 = ((f32[512]{0:T(512)S(1)}, f32[512]{0:T(512)S(1)}, f32[512,128]{1,0:T(8,128)S(1)})) conditional(s32[]{:T(128)} %convert_element_type.135, (f32[512]{0:T(512)S(1)}, f32[512]{0:T(512)S(1)}, f32[512,128]{1,0:T(8,128)S(1)}) %tuple.170, (s32[]{:T(128)}, s32[512]{0:T(512)S(1)}, s32[128]{0:T(128)S(1)}, bf16[4,512,128]{2,1,0:T(8,128)(2,1)}, ...), branch_computations={%region_8.8_spmd, %region_9.11_spmd} | conditional | flops 137496064 | bytes 4119592 | solution.py:112
  176.4 2.9 %conditional.13 = ((f32[512]{0:T(512)S(1)}, f32[512]{0:T(512)S(1)}, f32[512,128]{1,0:T(8,128)S(1)})) conditional(s32[]{:T(128)} %convert_element_type.135, (f32[512]{0:T(512)S(1)}, f32[512]{0:T(512)S(1)}, f32[512,128]{1,0:T(8,128)S(1)}) %tuple.170, (s32[]{:T(128)}, s32[512]{0:T(512)S(1)}, s32[128]{0:T(128)S(1)}, bf16[4,512,128]{2,1,0:T(8,128)(2,1)}, ...), branch_computations={%region_8.8_spmd, %region_9.11_spmd} | conditional | flops 137496064 | bytes 4119592 | solution.py:112
  179.7 18.4 %while.99 = (s32[]{:T(128)}, f32[512]{0:T(512)S(1)}, f32[512]{0:T(512)S(1)}, f32[512,128]{1,0:T(8,128)S(1)}, s32[4]{0:T(128)S(1)}, /*index=5*/s32[]{:T(128)}, bf...) while((s32[]{:T(128)}, f32[512]{0:T(512)S(1)}, ...), condition=%wide.region_24.25_spmd.clone, body=%wide.region_19.24_spmd.clone.sunk | while | flops 137496064 | bytes 4121887 | solution.py:122
  181.4 2.8 %conditional.15 = ((f32[512]{0:T(512)S(1)}, f32[512]{0:T(512)S(1)}, f32[512,128]{1,0:T(8,128)S(1)})) conditional(s32[]{:T(128)} %convert_element_type.137, (f32[512]{0:T(512)S(1)}, f32[512]{0:T(512)S(1)}, f32[512,128]{1,0:T(8,128)S(1)}) %tuple.176, (s32[]{:T(128)}, s32[512]{0:T(512)S(1)}, s32[128]{0:T(128)S(1)}, bf16[4,512,128]{2,1,0:T(8,128)(2,1)}, ...), branch_computations={%region_20.20_spmd, %region_21.23_spmd} | conditional | flops 137496064 | bytes 4119592 | solution.py:112
  186.0 2.8 %conditional.15 = ((f32[512]{0:T(512)S(1)}, f32[512]{0:T(512)S(1)}, f32[512,128]{1,0:T(8,128)S(1)})) conditional(s32[]{:T(128)} %convert_element_type.137, (f32[512]{0:T(512)S(1)}, f32[512]{0:T(512)S(1)}, f32[512,128]{1,0:T(8,128)S(1)}) %tuple.176, (s32[]{:T(128)}, s32[512]{0:T(512)S(1)}, s32[128]{0:T(128)S(1)}, bf16[4,512,128]{2,1,0:T(8,128)(2,1)}, ...), branch_computations={%region_20.20_spmd, %region_21.23_spmd} | conditional | flops 137496064 | bytes 4119592 | solution.py:112
  190.6 2.8 %conditional.15 = ((f32[512]{0:T(512)S(1)}, f32[512]{0:T(512)S(1)}, f32[512,128]{1,0:T(8,128)S(1)})) conditional(s32[]{:T(128)} %convert_element_type.137, (f32[512]{0:T(512)S(1)}, f32[512]{0:T(512)S(1)}, f32[512,128]{1,0:T(8,128)S(1)}) %tuple.176, (s32[]{:T(128)}, s32[512]{0:T(512)S(1)}, s32[128]{0:T(128)S(1)}, bf16[4,512,128]{2,1,0:T(8,128)(2,1)}, ...), branch_computations={%region_20.20_spmd, %region_21.23_spmd} | conditional | flops 137496064 | bytes 4119592 | solution.py:112
  195.2 2.8 %conditional.15 = ((f32[512]{0:T(512)S(1)}, f32[512]{0:T(512)S(1)}, f32[512,128]{1,0:T(8,128)S(1)})) conditional(s32[]{:T(128)} %convert_element_type.137, (f32[512]{0:T(512)S(1)}, f32[512]{0:T(512)S(1)}, f32[512,128]{1,0:T(8,128)S(1)}) %tuple.176, (s32[]{:T(128)}, s32[512]{0:T(512)S(1)}, s32[128]{0:T(128)S(1)}, bf16[4,512,128]{2,1,0:T(8,128)(2,1)}, ...), branch_computations={%region_20.20_spmd, %region_21.23_spmd} | conditional | flops 137496064 | bytes 4119592 | solution.py:112
  (270 shorter events, 61.8 us)
Async XLA Ops:
  6.5 24.7 %all-gather.3.cloned.1.call-start = ((), (), s32[]{:S(2)}) async-start(), calls=%async_computation | async-start | bytes 1572864 | tf_op jit(solution)/shard_map/all_gather | solution.py:149
  7.3 109.3 %all-gather.5.cloned.1.call-start = ((), (), s32[]{:S(2)}) async-start(), calls=%async_computation.1 | async-start | bytes 2228224 | tf_op jit(solution)/shard_map/all_gather | solution.py:87
  34.4 27.4 %copy-start = (bf16[128,4096]{1,0:T(8,128)(2,1)S(1)}, bf16[128,4096]{1,0:T(8,128)(2,1)}, u32[]{:S(2)}) copy-start(bf16[128,4096]{1,0:T(8,128)(2,1)} %all-gather.3.cloned.1.call-done) | copy-start | bytes 3145732
  35.1 3.8 %collective-permute-start = (bf16[128,512]{1,0:T(8,128)(2,1)S(1)}, bf16[128,512]{1,0:T(8,128)(2,1)S(1)}, u32[]{:S(2)}, u32[]{:S(2)}) collective-permute-start(bf16[128,512]{1,0:T(8,128)(2,1)S(1)} %bitcast.127), channel_id=1, source_target_pairs={{0,2},{2,4},{4,6},{6,8},{8,10},{10,12},{12,14},{14,16},{16,18},{18... | collective-permute-start | bytes 393224 | tf_op jit(solution)/shard_map/ppermute | solution.py:25
  38.8 4.4 %collective-permute-start.1 = (bf16[128,512]{1,0:T(8,128)(2,1)S(1)}, bf16[128,512]{1,0:T(8,128)(2,1)S(1)}, u32[]{:S(2)}, u32[]{:S(2)}) collective-permute-start(bf16[128,512]{1,0:T(8,128)(2,1)S(1)} %collective-permute-done), channel_id=1, source_target_pairs={{0,2},{2,4},{4,6},{6,8},{8,10},{10,12},{12,14},{14,16},{16,18},{18... | collective-permute-start | bytes 393224 | tf_op jit(solution)/shard_map/ppermute | solution.py:25
  41.3 5.8 %collective-permute-start.8 = (bf16[128,512]{1,0:T(8,128)(2,1)S(1)}, bf16[128,512]{1,0:T(8,128)(2,1)S(1)}, u32[]{:S(2)}, u32[]{:S(2)}) collective-permute-start(bf16[128,512]{1,0:T(8,128)(2,1)S(1)} %bitcast.128), channel_id=1, source_target_pairs={{2,0},{4,2},{6,4},{8,6},{10,8},{12,10},{14,12},{16,14},{18,16},{20... | collective-permute-start | bytes 393224 | tf_op jit(solution)/shard_map/ppermute | solution.py:27
  43.2 4.4 %collective-permute-start.2 = (bf16[128,512]{1,0:T(8,128)(2,1)S(1)}, bf16[128,512]{1,0:T(8,128)(2,1)S(1)}, u32[]{:S(2)}, u32[]{:S(2)}) collective-permute-start(bf16[128,512]{1,0:T(8,128)(2,1)S(1)} %collective-permute-done.1), channel_id=1, source_target_pairs={{0,2},{2,4},{4,6},{6,8},{8,10},{10,12},{12,14},{14,16},{16,18},{18... | collective-permute-start | bytes 393224 | tf_op jit(solution)/shard_map/ppermute | solution.py:25
  47.1 5.4 %collective-permute-start.9 = (bf16[128,512]{1,0:T(8,128)(2,1)S(1)}, bf16[128,512]{1,0:T(8,128)(2,1)S(1)}, u32[]{:S(2)}, u32[]{:S(2)}) collective-permute-start(bf16[128,512]{1,0:T(8,128)(2,1)S(1)} %collective-permute-done.8), channel_id=1, source_target_pairs={{2,0},{4,2},{6,4},{8,6},{10,8},{12,10},{14,12},{16,14},{18,16},{20... | collective-permute-start | bytes 393224 | tf_op jit(solution)/shard_map/ppermute | solution.py:27
  47.6 5.1 %collective-permute-start.3 = (bf16[128,512]{1,0:T(8,128)(2,1)S(1)}, bf16[128,512]{1,0:T(8,128)(2,1)S(1)}, u32[]{:S(2)}, u32[]{:S(2)}) collective-permute-start(bf16[128,512]{1,0:T(8,128)(2,1)S(1)} %collective-permute-done.2), channel_id=1, source_target_pairs={{0,2},{2,4},{4,6},{6,8},{8,10},{10,12},{12,14},{14,16},{16,18},{18... | collective-permute-start | bytes 393224 | tf_op jit(solution)/shard_map/ppermute | solution.py:25
  52.5 5.4 %collective-permute-start.10 = (bf16[128,512]{1,0:T(8,128)(2,1)S(1)}, bf16[128,512]{1,0:T(8,128)(2,1)S(1)}, u32[]{:S(2)}, u32[]{:S(2)}) collective-permute-start(bf16[128,512]{1,0:T(8,128)(2,1)S(1)} %collective-permute-done.9), channel_id=1, source_target_pairs={{2,0},{4,2},{6,4},{8,6},{10,8},{12,10},{14,12},{16,14},{18,16},{20... | collective-permute-start | bytes 393224 | tf_op jit(solution)/shard_map/ppermute | solution.py:27
  52.7 5.4 %collective-permute-start.4 = (bf16[128,512]{1,0:T(8,128)(2,1)S(1)}, bf16[128,512]{1,0:T(8,128)(2,1)S(1)}, u32[]{:S(2)}, u32[]{:S(2)}) collective-permute-start(bf16[128,512]{1,0:T(8,128)(2,1)S(1)} %collective-permute-done.3), channel_id=1, source_target_pairs={{0,2},{2,4},{4,6},{6,8},{8,10},{10,12},{12,14},{14,16},{16,18},{18... | collective-permute-start | bytes 393224 | tf_op jit(solution)/shard_map/ppermute | solution.py:25
  57.9 7.6 %collective-permute-start.11 = (bf16[128,512]{1,0:T(8,128)(2,1)S(1)}, bf16[128,512]{1,0:T(8,128)(2,1)S(1)}, u32[]{:S(2)}, u32[]{:S(2)}) collective-permute-start(bf16[128,512]{1,0:T(8,128)(2,1)S(1)} %collective-permute-done.10), channel_id=1, source_target_pairs={{2,0},{4,2},{6,4},{8,6},{10,8},{12,10},{14,12},{16,14},{18,16},{20... | collective-permute-start | bytes 393224 | tf_op jit(solution)/shard_map/ppermute | solution.py:27
  58.1 7.3 %copy-start.5 = (bf16[128,512]{1,0:T(8,128)(2,1)}, bf16[128,512]{1,0:T(8,128)(2,1)S(1)}, u32[]{:S(2)}) copy-start(bf16[128,512]{1,0:T(8,128)(2,1)S(1)} %collective-permute-done.4) | copy-start | bytes 393220
  58.1 8.2 %collective-permute-start.5 = (bf16[128,512]{1,0:T(8,128)(2,1)S(1)}, bf16[128,512]{1,0:T(8,128)(2,1)S(1)}, u32[]{:S(2)}, u32[]{:S(2)}) collective-permute-start(bf16[128,512]{1,0:T(8,128)(2,1)S(1)} %collective-permute-done.4), channel_id=1, source_target_pairs={{0,2},{2,4},{4,6},{6,8},{8,10},{10,12},{12,14},{14,16},{16,18},{18... | collective-permute-start | bytes 393224 | tf_op jit(solution)/shard_map/ppermute | solution.py:25
  65.5 14.5 %copy-start.3 = (bf16[128,512]{1,0:T(8,128)(2,1)}, bf16[128,512]{1,0:T(8,128)(2,1)S(1)}, u32[]{:S(2)}) copy-start(bf16[128,512]{1,0:T(8,128)(2,1)S(1)} %collective-permute-done.11) | copy-start | bytes 393220
  65.5 14.7 %collective-permute-start.12 = (bf16[128,512]{1,0:T(8,128)(2,1)S(1)}, bf16[128,512]{1,0:T(8,128)(2,1)S(1)}, u32[]{:S(2)}, u32[]{:S(2)}) collective-permute-start(bf16[128,512]{1,0:T(8,128)(2,1)S(1)} %collective-permute-done.11), channel_id=1, source_target_pairs={{2,0},{4,2},{6,4},{8,6},{10,8},{12,10},{14,12},{16,14},{18,16},{20... | collective-permute-start | bytes 393224 | tf_op jit(solution)/shard_map/ppermute | solution.py:27
  66.4 13.6 %copy-start.7 = (bf16[128,512]{1,0:T(8,128)(2,1)}, bf16[128,512]{1,0:T(8,128)(2,1)S(1)}, u32[]{:S(2)}) copy-start(bf16[128,512]{1,0:T(8,128)(2,1)S(1)} %collective-permute-done.5) | copy-start | bytes 393220
  66.4 13.9 %collective-permute-start.6 = (bf16[128,512]{1,0:T(8,128)(2,1)S(1)}, bf16[128,512]{1,0:T(8,128)(2,1)S(1)}, u32[]{:S(2)}, u32[]{:S(2)}) collective-permute-start(bf16[128,512]{1,0:T(8,128)(2,1)S(1)} %collective-permute-done.5), channel_id=1, source_target_pairs={{0,2},{2,4},{4,6},{6,8},{8,10},{10,12},{12,14},{14,16},{16,18},{18... | collective-permute-start | bytes 393224 | tf_op jit(solution)/shard_map/ppermute | solution.py:25
  80.2 8.1 %collective-permute-start.13 = (bf16[128,512]{1,0:T(8,128)(2,1)S(1)}, bf16[128,512]{1,0:T(8,128)(2,1)S(1)}, u32[]{:S(2)}, u32[]{:S(2)}) collective-permute-start(bf16[128,512]{1,0:T(8,128)(2,1)S(1)} %collective-permute-done.12), channel_id=1, source_target_pairs={{2,0},{4,2},{6,4},{8,6},{10,8},{12,10},{14,12},{16,14},{18,16},{20... | collective-permute-start | bytes 393224 | tf_op jit(solution)/shard_map/ppermute | solution.py:27
  80.3 8.0 %collective-permute-start.7 = (bf16[128,512]{1,0:T(8,128)(2,1)S(1)}, bf16[128,512]{1,0:T(8,128)(2,1)S(1)}, u32[]{:S(2)}, u32[]{:S(2)}) collective-permute-start(bf16[128,512]{1,0:T(8,128)(2,1)S(1)} %collective-permute-done.6), channel_id=1, source_target_pairs={{0,2},{2,4},{4,6},{6,8},{8,10},{10,12},{12,14},{14,16},{16,18},{18... | collective-permute-start | bytes 393224 | tf_op jit(solution)/shard_map/ppermute | solution.py:25
  85.5 2.8 %copy-start.8 = (bf16[128,512]{1,0:T(8,128)(2,1)S(1)}, bf16[128,512]{1,0:T(8,128)(2,1)}, u32[]{:S(2)}) copy-start(bf16[128,512]{1,0:T(8,128)(2,1)} %copy-done.7) | copy-start | bytes 393220
  85.5 2.9 %copy-start.6 = (bf16[128,512]{1,0:T(8,128)(2,1)S(1)}, bf16[128,512]{1,0:T(8,128)(2,1)}, u32[]{:S(2)}) copy-start(bf16[128,512]{1,0:T(8,128)(2,1)} %copy-done.5) | copy-start | bytes 393220
  86.0 2.5 %copy-start.4 = (bf16[128,512]{1,0:T(8,128)(2,1)S(1)}, bf16[128,512]{1,0:T(8,128)(2,1)}, u32[]{:S(2)}) copy-start(bf16[128,512]{1,0:T(8,128)(2,1)} %copy-done.3) | copy-start | bytes 393220
  88.3 6.6 %collective-permute-start.14 = (bf16[128,512]{1,0:T(8,128)(2,1)S(1)}, bf16[128,512]{1,0:T(8,128)(2,1)S(1)}, u32[]{:S(2)}, u32[]{:S(2)}) collective-permute-start(bf16[128,512]{1,0:T(8,128)(2,1)S(1)} %collective-permute-done.13), channel_id=1, source_target_pairs={{2,0},{4,2},{6,4},{8,6},{10,8},{12,10},{14,12},{16,14},{18,16},{20... | collective-permute-start | bytes 393224 | tf_op jit(solution)/shard_map/ppermute | solution.py:27
  123.3 18.5 %copy-start.2 = (bf16[2048,1,128]{2,1,0:T(2,128)(2,1)S(1)}, bf16[2048,1,128]{2,1,0:T(2,128)(2,1)}, u32[]{:S(2)}) copy-start(bf16[2048,1,128]{2,1,0:T(2,128)(2,1)} %get-tuple-element.1018) | copy-start | bytes 1572868
  141.9 18.5 %copy-start.1 = (bf16[2048,1,128]{2,1,0:T(2,128)(2,1)S(1)}, bf16[2048,1,128]{2,1,0:T(2,128)(2,1)}, u32[]{:S(2)}) copy-start(bf16[2048,1,128]{2,1,0:T(2,128)(2,1)} %get-tuple-element.1019) | copy-start | bytes 1572868
Sparse Core Ops, SparseCore 0:
  8.9 22.2 all-gather.2
  65.6 50.8 all-gather.4
